TPU v7x, 32 devices: a whole 2x2x4 slice. The times are simulated.
32 devices in a mesh: groups: 2 (over y), dp: 4 (over z), section: 2 (over x), tensor: 2 (over core).
Axes of the slice: x: 2, y: 2, z: 4, core: 2. Of those that a mesh axis runs over, the one named last changes fastest.
Arguments:
- cotangent: bfloat16 [2, 1024, 2048], P('section', ('groups', 'dp')), parts along dimension 1, may hold values from -6 to 6
- routes: int32 [2, 8, 2], P('section', ('groups', 'dp')), parts along dimension 1, may hold values from 0 to 3, all different within a row
- gate_values: float32 [2, 1024, 2], P('section', ('groups', 'dp')), parts along dimension 1, may hold values from 0.1 to 0.9
- up_weight: bfloat16 [2, 4, 2048, 7168], P('section', 'dp', None, 'tensor'), may hold values from -0.125 to 0.125
- down_weight: bfloat16 [2, 4, 7168, 2048], P('section', 'dp', 'tensor'), may hold values from -0.0625 to 0.0625
- pre_activation: bfloat16 [2, 8, 4, 128, 7168], P('section', ('groups', 'dp'), None, None, 'tensor'), parts along dimension 1, may hold values from -6 to 6
- input_sketch: float32 [2, 1024, 64], P('section', ('groups', 'dp')), parts along dimension 1, may hold values from -6 to 6
- model_sketch: bfloat16 [2, 2048, 64], P('section'), may hold values from -0.125 to 0.125
- hidden_sketch: bfloat16 [2, 4, 7168, 64], P('section', 'dp', 'tensor'), may hold values from -0.0625 to 0.0625
- lengths: int32 [2, 8, 4], P('section', ('groups', 'dp')), parts along dimension 1, may hold values from 1 to 64, 128 in all within a row
Outputs:
- handed: bfloat16 [2, 1024, 2048], P('section', ('groups', 'dp')), parts along dimension 1
- features: float32 [2, 32, 64, 128], P('section', ('groups', 'dp')), parts along dimension 1
There are 2 independent parts, one for each index of `groups`. A program takes and returns all parts, laid end to end along the dimension named above; an argument that names none is the same for every part. Nothing has to cross between parts.
Inputs may be any that keep to these rules, and one draw needn't show every extreme that they name: `routes`: the two experts of a block differ. `lengths`: each row of counts sums to 128, and its largest is 64.
All inputs are finite; a program needn't handle non-finite values.
Results may differ from a plain program's by a relative error of at most 0.0037.
Values may be sent and summed in bfloat16 or wider, within the bound.
A program may use at most 128 MiB of HBM per device.

v0:
```python
import functools

import jax
import jax.numpy as jnp
from jax import lax
from jax.experimental import pallas as pl
from jax.experimental.pallas import tpu as pltpu
from jax.sharding import PartitionSpec as P

EXPERTS = 4
F32 = jnp.float32
BF16 = jnp.bfloat16
NT = (((1,), (1,)), ((), ()))


def tile_of(extent, most):
    return max(t for t in range(128, most + 1, 128) if extent % t == 0)


def xor(d, k, n):
    if n & (n - 1):
        return (d + k) % n
    out, bit = 0, 1
    while bit < n:
        b = (d // bit) % 2
        out = out + ((1 - b) if k & bit else b) * bit
        bit *= 2
    return out


def kernel(
    n,
    sections,
    group,
    th,
    tn,
    cot_hbm,
    routes_ref,
    gates_ref,
    up_hbm,
    down_hbm,
    pre_hbm,
    insk_ref,
    model_ref,
    sketch_ref,
    len_ref,
    hand_out,
    feat_out,
    cot_all,
    wt_own,
    wt_all,
    slope_v,
    down_v2,
    up_v,
    down_v,
    pre_v,
    rows_v,
    gp_v,
    acc_v,
    mine_v,
    sk_v,
    xsend,
    xrecv,
    ssend,
    srecv,
    osend,
    orecv,
    tsend,
    trecv,
    cot_next,
    sk_sum,
    down_sem,
    up_sem,
    pre_sem,
    own_sem,
    ag_send,
    ag_recv,
    wt_send,
    wt_recv,
    fw_send,
    fw_recv,
    cn_send,
    cn_recv,
    x_send,
    x_recv,
    s_send,
    s_recv,
    o_send,
    o_recv,
    t_send,
    t_recv,
    h_send,
    h_recv,
    k_send,
    k_recv,
):
    tok, width = cot_hbm.shape
    half = tok // 2
    hidden_cols = up_hbm.shape[1]
    rank = insk_ref.shape[0]
    d = lax.axis_index("dp")
    s = lax.axis_index("section")
    c = lax.axis_index("tensor")
    pc = 1 - c
    below = (s + sections - 1) % sections
    above = (s + 1) % sections
    n_groups = n // group
    n_th = hidden_cols // th
    n_tn = width // tn
    if n >= 4 and n & (n - 1) == 0:
        order = [0] + list(range(n // 2, n)) + list(range(1, n // 2))
    else:
        order = list(range(n))
    blocks = [xor(d, k, n) for k in order]
    mine_rows = pl.ds(pl.multiple_of(c * half, half), half)
    other_rows = pl.ds(pl.multiple_of(pc * half, half), half)

    def remote(src, dst, ssem, rsem, **to):
        return pltpu.make_async_remote_copy(
            src_ref=src,
            dst_ref=dst,
            send_sem=ssem,
            recv_sem=rsem,
            device_id=to,
            device_id_type=pl.DeviceIdType.MESH,
        )

    own_copy = pltpu.make_async_copy(cot_hbm, cot_all.at[d], own_sem)
    own_copy.start()

    def pre_copy(b, i):
        return pltpu.make_async_copy(pre_hbm.at[b], pre_v.at[b], pre_sem.at[i])

    def down_copy(t):
        rows = pl.ds(pl.multiple_of(t * th, th), th)
        return pltpu.make_async_copy(down_hbm.at[rows], down_v.at[rows], down_sem.at[t])

    def up_copy(t):
        rows = pl.ds(pl.multiple_of(t * tn, tn), tn)
        return pltpu.make_async_copy(up_hbm.at[rows], up_v.at[rows], up_sem.at[t])

    for i in range(n):
        pre_copy(blocks[i], i).start()
    for t in range(n_th):
        down_copy(t).start()
    for t in range(n_tn):
        up_copy(t).start()

    block_rows = routes_ref.shape[0]
    token_block = lax.broadcasted_iota(jnp.int32, (8, tok), 1) // (tok // block_rows)
    for p in range(n):
        expert = p // (n // EXPERTS)
        weight = jnp.zeros((8, tok), F32)
        for q in range(block_rows):
            for k in range(2):
                share = jnp.where(token_block == q, gates_ref[k : k + 1, :], 0.0)
                weight += jnp.where(routes_ref[q, k] == expert, share, 0.0)
        wt_own[p] = weight

    barrier = pltpu.get_barrier_semaphore()
    greet = [{"tensor": pc}]
    greet += [{"dp": blocks[i]} for i in range(1, n)]
    greet += [{"section": below, "dp": blocks[i]} for i in range(n)]
    if sections > 2:
        greet += [{"section": above, "dp": blocks[i]} for i in range(n)]
    for to in greet:
        pl.semaphore_signal(barrier, inc=1, device_id=to, device_id_type=pl.DeviceIdType.MESH)
    pl.semaphore_wait(barrier, len(greet))

    def ag_copy(i, source):
        return remote(
            cot_hbm.at[mine_rows],
            cot_all.at[source, mine_rows],
            ag_send.at[i],
            ag_recv.at[source],
            dp=blocks[i],
        )

    def wt_copy(i, source):
        return remote(
            wt_own.at[blocks[i]], wt_all.at[source], wt_send.at[i], wt_recv.at[source], dp=blocks[i]
        )

    cn_copy = remote(cot_hbm.at[mine_rows], cot_next, cn_send, cn_recv, section=below)
    for i in range(1, n):
        wt_copy(i, d).start()
        ag_copy(i, d).start()
    cn_copy.start()

    def fw_copy(i, rows):
        b = blocks[i]
        return remote(
            cot_all.at[b, rows], cot_all.at[b, rows], fw_send.at[b], fw_recv.at[b], tensor=pc
        )

    def forward(i):
        if i:
            ag_copy(i, blocks[i]).wait_recv()
            fw_copy(i, mine_rows).start()

    own_copy.wait()
    out_vec_t = lax.dot_general(
        model_ref[...], cot_all[d], NT, preferred_element_type=F32
    )
    wt_all[d] = wt_own[d]
    eye = lax.broadcasted_iota(jnp.int32, (tok, tok), 0) == lax.broadcasted_iota(
        jnp.int32, (tok, tok), 1
    )

    def x_copy(g, t):
        return remote(xsend.at[g, t], xrecv.at[g, t], x_send.at[g, t], x_recv.at[g, t], tensor=pc)

    def s_copy(g):
        return remote(ssend.at[g], srecv.at[g], s_send.at[g], s_recv.at[g], tensor=pc)

    def o_copy(i, t, b, source):
        return remote(
            osend.at[i, t],
            orecv.at[source, t],
            o_send.at[i, t],
            o_recv.at[source, t],
            section=below,
            dp=b,
        )

    def t_copy(i, b, source):
        return remote(tsend.at[i], trecv.at[source], t_send.at[i], t_recv.at[source], dp=b)

    for i in range(n):
        pre_copy(blocks[i], i).wait()
    down_v2[...] = jnp.zeros_like(down_v2)

    def ahead(t, carry):
        rows = pl.ds(pl.multiple_of(t * th, th), th)
        sk = sketch_ref[:, rows]
        for b in range(n):
            pre = pre_v[b, :, rows].astype(F32)
            sig = jax.nn.sigmoid(pre)
            hid = (pre * sig).astype(BF16)
            slope_v[b, :, rows] = sig * (1.0 + pre * (1.0 - sig))
            down_v2[b] += lax.dot_general(hid, sk, NT, preferred_element_type=F32)
        return carry

    lax.fori_loop(0, n_th, ahead, 0)
    for i in range(group):
        forward(i)
    for g in range(n_groups):
        members = list(range(g * group, (g + 1) * group))
        for j, i in enumerate(members):
            b = blocks[i]
            if i:
                fw_copy(i, other_rows).wait_recv()
                wt_copy(i, b).wait_recv()
            row = wt_all[b][0:1, :]
            col = jnp.sum(jnp.where(eye, jnp.broadcast_to(row, (tok, tok)), 0.0), axis=1, keepdims=True)
            at = slice(j * tok, (j + 1) * tok)
            rows_v[at, :] = (col * cot_all[b].astype(F32)).astype(BF16)
            sk_v[at, :] = jnp.concatenate([down_v2[b] * col, jnp.zeros((tok, rank), F32)], axis=1)

        def first(t, carry, g=g, members=members):
            if g == 0:
                down_copy(t).wait()
            rows = pl.ds(pl.multiple_of(t * th, th), th)
            gh = lax.dot_general(rows_v[...], down_v[rows, :], NT, preferred_element_type=F32)
            for j, i in enumerate(members):
                at = slice(j * tok, (j + 1) * tok)
                gp_v[at, rows] = (gh[at] * slope_v[blocks[i], :, rows]).astype(BF16)
            return carry

        lax.fori_loop(0, n_th, first, 0)
        sk_v[:, rank:] = lax.dot_general(
            gp_v[...], sketch_ref[...], NT, preferred_element_type=F32
        )
        for j in range(group):
            ssend[g, j * half : (j + 1) * half, :] = sk_v[
                pl.ds(pl.multiple_of(j * tok + pc * half, half), half), :
            ]
        s_copy(g).start()

        far_first = members[::-1] if g == 0 else members

        def pass_on(t, g=g, members=members, far_first=far_first):
            x_copy(g, t).wait_recv()
            cols = pl.ds(pl.multiple_of(t * tn, tn), tn)
            for i in far_first:
                j = members.index(i)
                at = slice(j * half, (j + 1) * half)
                osend[i, t] = (mine_v[at, cols] + xrecv[g, t, at, :].astype(F32)).astype(BF16)
                o_copy(i, t, blocks[i], d).start()

        def second(t, carry, g=g, pass_on=pass_on):
            if g == 0:
                up_copy(t).wait()
            rows = pl.ds(pl.multiple_of(t * tn, tn), tn)
            acc_v[...] = lax.dot_general(gp_v[...], up_v[rows, :], NT, preferred_element_type=F32)
            for j in range(group):
                at = slice(j * half, (j + 1) * half)
                mine_v[at, rows] = acc_v[pl.ds(pl.multiple_of(j * tok + c * half, half), half), :]
                xsend[g, t, at, :] = acc_v[
                    pl.ds(pl.multiple_of(j * tok + pc * half, half), half), :
                ].astype(BF16)
            x_copy(g, t).start()

            @pl.when(t > 0)
            def _():
                pass_on(t - 1)

            return carry

        lax.fori_loop(0, n_tn, second, 0)
        if g + 1 < n_groups:
            for j in range(group):
                forward((g + 1) * group + j)
        pass_on(n_tn - 1)
        s_copy(g).wait_recv()
        for j, i in enumerate(members):
            at = slice(j * half, (j + 1) * half)
            total = sk_v[pl.ds(pl.multiple_of(j * tok + c * half, half), half), :] + srecv[g, at, :]
            if i:
                tsend[i] = total
                t_copy(i, blocks[i], d).start()
            else:
                sk_sum[mine_rows, :] = total
    for i in range(1, n):
        t_copy(i, blocks[i], blocks[i]).wait_recv()
        sk_sum[mine_rows, :] += trecv[blocks[i]]

    def k_copy(rows):
        return remote(sk_sum.at[rows], sk_sum.at[rows], k_send, k_recv, tensor=pc)

    k_copy(mine_rows).start()
    cn_copy.wait_recv()
    def h_copy(t, rows):
        part = hand_out.at[rows, pl.ds(t * tn, tn)]
        return remote(part, part, h_send.at[t], h_recv.at[t], tensor=pc)

    for t in range(n_tn):
        cols = slice(t * tn, (t + 1) * tn)
        total = cot_next[:, cols].astype(F32)
        for i in range(n):
            o_copy(i, t, blocks[i], blocks[i]).wait_recv()
            total = total + orecv[blocks[i], t].astype(F32)
        hand_out[mine_rows, cols] = total.astype(BF16)
        h_copy(t, mine_rows).start()

    k_copy(other_rows).wait_recv()
    sk = sk_sum[...]
    up_vec_t = sk.T[rank:, :]
    position = lax.broadcasted_iota(jnp.int32, (rank, tok), 1)
    left, right = [], []
    begin = jnp.int32(0)
    for e in range(len_ref.shape[0]):
        end = begin + len_ref[e]
        member = (position >= begin) & (position < end)
        left.append(jnp.where(member, out_vec_t, 0.0))
        right.append(jnp.where(member, up_vec_t, 0.0))
        begin = end
    exact = functools.partial(
        jnp.dot, preferred_element_type=F32, precision=lax.Precision.HIGHEST
    )
    down_feat = exact(jnp.concatenate(left, axis=0), sk[:, :rank])
    up_feat = lax.dot_general(
        jnp.concatenate(right, axis=0),
        insk_ref[...],
        NT,
        preferred_element_type=F32,
        precision=lax.Precision.HIGHEST,
    )
    feat_out[...] = jnp.concatenate([down_feat, up_feat], axis=1)

    for t in range(n_tn):
        h_copy(t, other_rows).wait_recv()
        h_copy(t, mine_rows).wait_send()
    for i in range(1, n):
        wt_copy(i, d).wait_send()
        ag_copy(i, d).wait_send()
        fw_copy(i, mine_rows).wait_send()
        t_copy(i, blocks[i], d).wait_send()
    for i in range(n):
        for t in range(n_tn):
            o_copy(i, t, blocks[i], d).wait_send()
    for g in range(n_groups):
        s_copy(g).wait_send()
        for t in range(n_tn):
            x_copy(g, t).wait_send()
    cn_copy.wait_send()
    k_copy(mine_rows).wait_send()


GROUP = 2


def per_device(
    cotangent,
    routes,
    gate_values,
    up_weight,
    down_weight,
    pre_activation,
    input_sketch,
    model_sketch,
    hidden_sketch,
    lengths,
):
    n = lax.axis_size("dp")
    sections = lax.axis_size("section")
    tok, width = cotangent.shape[1:]
    rank = model_sketch.shape[2]
    hidden_cols = up_weight.shape[3]
    examples = lengths.shape[2]
    group = GROUP
    half = tok // 2
    m = group * tok
    th = tile_of(hidden_cols, 512)
    tn = tile_of(width, 512)
    n_th, n_tn, n_g = hidden_cols // th, width // tn, n // group
    dma = pltpu.SemaphoreType.DMA
    vmem = pl.BlockSpec(memory_space=pltpu.VMEM)
    hbm = pl.BlockSpec(memory_space=pl.ANY)
    hand, feat = pl.pallas_call(
        functools.partial(kernel, n, sections, group, th, tn),
        out_shape=(
            jax.ShapeDtypeStruct((tok, width), BF16),
            jax.ShapeDtypeStruct((examples * rank, 2 * rank), F32),
        ),
        in_specs=[
            hbm,
            pl.BlockSpec(memory_space=pltpu.SMEM),
            vmem,
            hbm,
            hbm,
            hbm,
            vmem,
            vmem,
            vmem,
            pl.BlockSpec(memory_space=pltpu.SMEM),
        ],
        out_specs=(vmem, vmem),
        scratch_shapes=[
            pltpu.VMEM((n, tok, width), BF16),
            pltpu.VMEM((n, 8, tok), F32),
            pltpu.VMEM((n, 8, tok), F32),
            pltpu.VMEM((n, tok, hidden_cols), F32),
            pltpu.VMEM((n, tok, rank), F32),
            pltpu.VMEM((width, hidden_cols), BF16),
            pltpu.VMEM((hidden_cols, width), BF16),
            pltpu.VMEM((n, tok, hidden_cols), BF16),
            pltpu.VMEM((m, width), BF16),
            pltpu.VMEM((m, hidden_cols), BF16),
            pltpu.VMEM((m, tn), F32),
            pltpu.VMEM((m // 2, width), F32),
            pltpu.VMEM((m, 2 * rank), F32),
            pltpu.VMEM((n_g, n_tn, m // 2, tn), BF16),
            pltpu.VMEM((n_g, n_tn, m // 2, tn), BF16),
            pltpu.VMEM((n_g, m // 2, 2 * rank), F32),
            pltpu.VMEM((n_g, m // 2, 2 * rank), F32),
            pltpu.VMEM((n, n_tn, half, tn), BF16),
            pltpu.VMEM((n, n_tn, half, tn), BF16),
            pltpu.VMEM((n, half, 2 * rank), F32),
            pltpu.VMEM((n, half, 2 * rank), F32),
            pltpu.VMEM((half, width), BF16),
            pltpu.VMEM((tok, 2 * rank), F32),
            dma((n_th,)),
            dma((n_tn,)),
            dma((n,)),
            dma(()),
            dma((n,)),
            dma((n,)),
            dma((n,)),
            dma((n,)),
            dma((n,)),
            dma((n,)),
            dma(()),
            dma(()),
            dma((n_g, n_tn)),
            dma((n_g, n_tn)),
            dma((n_g,)),
            dma((n_g,)),
            dma((n, n_tn)),
            dma((n, n_tn)),
            dma((n,)),
            dma((n,)),
            dma((n_tn,)),
            dma((n_tn,)),
            dma(()),
            dma(()),
        ],
        compiler_params=pltpu.CompilerParams(
            collective_id=0, has_side_effects=True, vmem_limit_bytes=63 * 1024 * 1024
        ),
        name="window",
    )(
        cotangent[0],
        routes[0],
        gate_values[0].T,
        up_weight[0, 0],
        down_weight[0, 0],
        pre_activation[0, 0],
        input_sketch[0].T,
        model_sketch[0].T,
        hidden_sketch[0, 0].T,
        lengths[0, 0],
    )
    return (hand[None], feat.reshape(1, examples, rank, 2 * rank))


def solution(mesh):
    in_specs = (
        P("section", ("groups", "dp"), None),
        P("section", ("groups", "dp"), None),
        P("section", ("groups", "dp"), None),
        P("section", "dp", None, "tensor"),
        P("section", "dp", "tensor", None),
        P("section", ("groups", "dp"), None, None, "tensor"),
        P("section", ("groups", "dp"), None),
        P("section", None, None),
        P("section", "dp", "tensor", None),
        P("section", ("groups", "dp"), None),
    )
    out_specs = (P("section", ("groups", "dp"), None), P("section", ("groups", "dp"), None, None))
    return jax.shard_map(
        per_device, mesh=mesh, in_specs=in_specs, out_specs=out_specs, check_vma=False
    )
```

profile of v0, /device:TPU:0, one launch (start us, length us, event | category | flops | bytes accessed | tf_op | source)
XLA Modules:
  0.0 71.8 jit_solution(6315283722048419601)
XLA Ops:
  0.6 67.7 %window.1 = (bf16[128,2048]{1,0:T(8,128)(2,1)}, f32[256,128]{1,0:T(8,128)}) custom-call(bf16[128,2048]{1,0:T(8,128)(2,1)} %bitcast.23, s32[1,2]{1,0:T(1,128)} %bitcast.30, f32[2,128]{1,0:T(2,128)} %bitcast.29, bf16[2048,3584]{1,0:T(8,128)(2,1)} %bitcast.20, bf16[3584,2048]{1,0:T(8,128)(2,1)} %bitcast.21, bf16[4,128,3584]{2,1,0:T(8,128)(2,1)} %bitcast.22, ...), custom_call_target="tpu_custom_call" | custom-call | tf_op jit(solution)/shard_map/window/pallas_call | solution.py:420
  68.3 1.9 %copy.14 = bf16[1,128,2048]{2,1,0:T(8,128)(2,1)} copy(bf16[1,128,2048]{2,1,0:T(8,128)(2,1)} %bitcast.24) | data formatting | bytes 1048576
  70.2 1.6 %copy.15 = f32[1,4,64,128]{3,2,1,0:T(8,128)} copy(f32[1,4,64,128]{3,2,1,0:T(8,128)} %bitcast.27) | data formatting | bytes 262144
where the time goes:
time: 72 us; the launch traced here: 71.8 us
  Pallas kernels  67.7 us (94%)
  local copies, waits for them, and re-layouts  3.45 us (5%)
    pallas_call x1, Pallas kernels, per_device(): pl.pallas_call(functools.partial(kernel, n, sections, group, th, tn), out...  67.7 us
    unnamed x2, local copies, waits for them, and re-layouts  3.45 us

commit v1 on v0

--- a/solution.py
+++ b/solution.py
@@ -17,14 +17,15 @@
     return max(t for t in range(128, most + 1, 128) if extent % t == 0)
 
 
-def xor(d, k, n):
-    if n & (n - 1):
-        return (d + k) % n
-    out, bit = 0, 1
-    while bit < n:
-        b = (d // bit) % 2
-        out = out + ((1 - b) if k & bit else b) * bit
-        bit *= 2
+def slots(d, n):
+    upper = d // (n // 2)
+    edge = d + upper * (n - 1 - 2 * d)
+    side = 1 - 2 * upper
+    out = [d]
+    for i in range(1, n):
+        near = (i + 1) // 2 if i % 2 else -(i // 2)
+        both = jnp.where(2 * edge >= i, 1, 0)
+        out.append(d + side * (both * near + (1 - both) * (i - edge)))
     return out
 
 
@@ -73,7 +74,8 @@
     up_sem,
     pre_sem,
     own_sem,
-    ag_send,
+    up_send,
+    dn_send,
     ag_recv,
     wt_send,
     wt_recv,
@@ -107,11 +109,7 @@
     n_groups = n // group
     n_th = hidden_cols // th
     n_tn = width // tn
-    if n >= 4 and n & (n - 1) == 0:
-        order = [0] + list(range(n // 2, n)) + list(range(1, n // 2))
-    else:
-        order = list(range(n))
-    blocks = [xor(d, k, n) for k in order]
+    blocks = slots(d, n)
     mine_rows = pl.ds(pl.multiple_of(c * half, half), half)
     other_rows = pl.ds(pl.multiple_of(pc * half, half), half)
 
@@ -167,36 +165,78 @@
         pl.semaphore_signal(barrier, inc=1, device_id=to, device_id_type=pl.DeviceIdType.MESH)
     pl.semaphore_wait(barrier, len(greet))
 
-    def ag_copy(i, source):
+    part = half // CHUNKS
+
+    def chunk(core, j):
+        return pl.ds(pl.multiple_of(core * half + j * part, part), part)
+
+    def line_copy(b, j, to, send):
+        rows = chunk(c, j)
         return remote(
-            cot_hbm.at[mine_rows],
-            cot_all.at[source, mine_rows],
-            ag_send.at[i],
-            ag_recv.at[source],
-            dp=blocks[i],
-        )
+            cot_all.at[b, rows], cot_all.at[b, rows], send.at[b, j], ag_recv.at[b, j], dp=to
+        )
+
+    def own_line(j, to, send):
+        rows = chunk(c, j)
+        return remote(
+            cot_hbm.at[rows], cot_all.at[d, rows], send.at[d, j], ag_recv.at[d, j], dp=to
+        )
+
+    def up_line(b, j):
+        return line_copy(b, j, jnp.minimum(d + 1, n - 1), up_send)
+
+    def down_line(b, j):
+        return line_copy(b, j, jnp.maximum(d - 1, 0), dn_send)
 
     def wt_copy(i, source):
         return remote(
             wt_own.at[blocks[i]], wt_all.at[source], wt_send.at[i], wt_recv.at[source], dp=blocks[i]
         )
 
+    def fw_copy(b, j, core):
+        rows = chunk(core, j)
+        return remote(
+            cot_all.at[b, rows], cot_all.at[b, rows], fw_send.at[b, j], fw_recv.at[b, j], tensor=pc
+        )
+
     cn_copy = remote(cot_hbm.at[mine_rows], cot_next, cn_send, cn_recv, section=below)
     for i in range(1, n):
         wt_copy(i, d).start()
-        ag_copy(i, d).start()
+
+    @pl.when(d < n - 1)
+    def _():
+        for j in range(CHUNKS):
+            own_line(j, d + 1, up_send).start()
+
+    @pl.when(d > 0)
+    def _():
+        for j in range(CHUNKS):
+            own_line(j, d - 1, dn_send).start()
+
     cn_copy.start()
 
-    def fw_copy(i, rows):
-        b = blocks[i]
-        return remote(
-            cot_all.at[b, rows], cot_all.at[b, rows], fw_send.at[b], fw_recv.at[b], tensor=pc
-        )
-
-    def forward(i):
-        if i:
-            ag_copy(i, blocks[i]).wait_recv()
-            fw_copy(i, mine_rows).start()
+    def arrive(k, chunks=range(CHUNKS)):
+        for j in chunks:
+
+            @pl.when(d >= k)
+            def _(j=j):
+                up_line(d - k, j).wait_recv()
+
+                @pl.when(d < n - 1)
+                def _():
+                    up_line(d - k, j).start()
+
+                fw_copy(d - k, j, c).start()
+
+            @pl.when(d + k < n)
+            def _(j=j):
+                down_line(d + k, j).wait_recv()
+
+                @pl.when(d > 0)
+                def _():
+                    down_line(d + k, j).start()
+
+                fw_copy(d + k, j, c).start()
 
     own_copy.wait()
     out_vec_t = lax.dot_general(
@@ -242,18 +282,21 @@
         return carry
 
     lax.fori_loop(0, n_th, ahead, 0)
-    for i in range(group):
-        forward(i)
+    arrived = 0
     for g in range(n_groups):
         members = list(range(g * group, (g + 1) * group))
-        for j, i in enumerate(members):
+        while arrived < min(members[-1], n - 1):
+            arrived += 1
+            arrive(arrived)
+        for m, i in enumerate(members):
             b = blocks[i]
             if i:
-                fw_copy(i, other_rows).wait_recv()
+                for j in range(CHUNKS):
+                    fw_copy(b, j, pc).wait_recv()
                 wt_copy(i, b).wait_recv()
             row = wt_all[b][0:1, :]
             col = jnp.sum(jnp.where(eye, jnp.broadcast_to(row, (tok, tok)), 0.0), axis=1, keepdims=True)
-            at = slice(j * tok, (j + 1) * tok)
+            at = slice(m * tok, (m + 1) * tok)
             rows_v[at, :] = (col * cot_all[b].astype(F32)).astype(BF16)
             sk_v[at, :] = jnp.concatenate([down_v2[b] * col, jnp.zeros((tok, rank), F32)], axis=1)
 
@@ -268,6 +311,9 @@
             return carry
 
         lax.fori_loop(0, n_th, first, 0)
+        if arrived < n - 1:
+            arrived += 1
+            arrive(arrived)
         sk_v[:, rank:] = lax.dot_general(
             gp_v[...], sketch_ref[...], NT, preferred_element_type=F32
         )
@@ -288,7 +334,18 @@
                 osend[i, t] = (mine_v[at, cols] + xrecv[g, t, at, :].astype(F32)).astype(BF16)
                 o_copy(i, t, blocks[i], d).start()
 
-        def second(t, carry, g=g, pass_on=pass_on):
+        def sketch_on(g=g, members=members):
+            s_copy(g).wait_recv()
+            for j, i in enumerate(members):
+                at = slice(j * half, (j + 1) * half)
+                total = sk_v[pl.ds(pl.multiple_of(j * tok + c * half, half), half), :] + srecv[g, at, :]
+                if i:
+                    tsend[i] = total
+                    t_copy(i, blocks[i], d).start()
+                else:
+                    sk_sum[mine_rows, :] = total
+
+        def second(t, carry, g=g, pass_on=pass_on, sketch_on=sketch_on):
             if g == 0:
                 up_copy(t).wait()
             rows = pl.ds(pl.multiple_of(t * tn, tn), tn)
@@ -305,22 +362,14 @@
             def _():
                 pass_on(t - 1)
 
+            @pl.when(t == 1)
+            def _():
+                sketch_on()
+
             return carry
 
         lax.fori_loop(0, n_tn, second, 0)
-        if g + 1 < n_groups:
-            for j in range(group):
-                forward((g + 1) * group + j)
         pass_on(n_tn - 1)
-        s_copy(g).wait_recv()
-        for j, i in enumerate(members):
-            at = slice(j * half, (j + 1) * half)
-            total = sk_v[pl.ds(pl.multiple_of(j * tok + c * half, half), half), :] + srecv[g, at, :]
-            if i:
-                tsend[i] = total
-                t_copy(i, blocks[i], d).start()
-            else:
-                sk_sum[mine_rows, :] = total
     for i in range(1, n):
         t_copy(i, blocks[i], blocks[i]).wait_recv()
         sk_sum[mine_rows, :] += trecv[blocks[i]]
@@ -329,20 +378,6 @@
         return remote(sk_sum.at[rows], sk_sum.at[rows], k_send, k_recv, tensor=pc)
 
     k_copy(mine_rows).start()
-    cn_copy.wait_recv()
-    def h_copy(t, rows):
-        part = hand_out.at[rows, pl.ds(t * tn, tn)]
-        return remote(part, part, h_send.at[t], h_recv.at[t], tensor=pc)
-
-    for t in range(n_tn):
-        cols = slice(t * tn, (t + 1) * tn)
-        total = cot_next[:, cols].astype(F32)
-        for i in range(n):
-            o_copy(i, t, blocks[i], blocks[i]).wait_recv()
-            total = total + orecv[blocks[i], t].astype(F32)
-        hand_out[mine_rows, cols] = total.astype(BF16)
-        h_copy(t, mine_rows).start()
-
     k_copy(other_rows).wait_recv()
     sk = sk_sum[...]
     up_vec_t = sk.T[rank:, :]
@@ -368,13 +403,25 @@
     )
     feat_out[...] = jnp.concatenate([down_feat, up_feat], axis=1)
 
+    cn_copy.wait_recv()
+    def h_copy(t, rows):
+        part = hand_out.at[rows, pl.ds(t * tn, tn)]
+        return remote(part, part, h_send.at[t], h_recv.at[t], tensor=pc)
+
+    for t in range(n_tn):
+        cols = slice(t * tn, (t + 1) * tn)
+        total = cot_next[:, cols].astype(F32)
+        for i in range(n):
+            o_copy(i, t, blocks[i], blocks[i]).wait_recv()
+            total = total + orecv[blocks[i], t].astype(F32)
+        hand_out[mine_rows, cols] = total.astype(BF16)
+        h_copy(t, mine_rows).start()
+
     for t in range(n_tn):
         h_copy(t, other_rows).wait_recv()
         h_copy(t, mine_rows).wait_send()
     for i in range(1, n):
         wt_copy(i, d).wait_send()
-        ag_copy(i, d).wait_send()
-        fw_copy(i, mine_rows).wait_send()
         t_copy(i, blocks[i], d).wait_send()
     for i in range(n):
         for t in range(n_tn):
@@ -383,11 +430,33 @@
         s_copy(g).wait_send()
         for t in range(n_tn):
             x_copy(g, t).wait_send()
+    for k in range(n):
+        for j in range(CHUNKS):
+
+            @pl.when(d >= k)
+            def _(k=k, j=j):
+                @pl.when(d < n - 1)
+                def _():
+                    up_line(d - k, j).wait_send()
+
+                if k:
+                    fw_copy(d - k, j, c).wait_send()
+
+            @pl.when(d + k < n)
+            def _(k=k, j=j):
+                @pl.when(d > 0)
+                def _():
+                    down_line(d + k, j).wait_send()
+
+                if k:
+                    fw_copy(d + k, j, c).wait_send()
+
     cn_copy.wait_send()
     k_copy(mine_rows).wait_send()
 
 
 GROUP = 2
+CHUNKS = 2
 
 
 def per_device(
@@ -464,12 +533,13 @@
             dma((n_tn,)),
             dma((n,)),
             dma(()),
+            dma((n, CHUNKS)),
+            dma((n, CHUNKS)),
+            dma((n, CHUNKS)),
             dma((n,)),
             dma((n,)),
-            dma((n,)),
-            dma((n,)),
-            dma((n,)),
-            dma((n,)),
+            dma((n, CHUNKS)),
+            dma((n, CHUNKS)),
             dma(()),
             dma(()),
             dma((n_g, n_tn)),

time: 72 us -> 68.4 us (0.950)
  Pallas kernels: 67.7 us -> 64.1 us
    pallas_call x1, Pallas kernels: 67.7 us -> 64.1 us  [per_device(): pl.pallas_call(functools.partial(kernel, n, sections, group, th, tn), out...]
where the time goes in v1:
time: 68.4 us; the launch traced here: 68.2 us
  Pallas kernels  64.1 us (94%)
  local copies, waits for them, and re-layouts  3.45 us (5%)
    pallas_call x1, Pallas kernels, per_device(): pl.pallas_call(functools.partial(kernel, n, sections, group, th, tn), out...  64.1 us
    unnamed x2, local copies, waits for them, and re-layouts  3.45 us

profile of v1, /device:TPU:0, one launch (start us, length us, event | category | flops | bytes accessed | tf_op | source)
XLA Modules:
  0.0 68.2 jit_solution(15410131384906696695)
XLA Ops:
  0.6 64.1 %window.1 = (bf16[128,2048]{1,0:T(8,128)(2,1)}, f32[256,128]{1,0:T(8,128)}) custom-call(bf16[128,2048]{1,0:T(8,128)(2,1)} %bitcast.23, s32[1,2]{1,0:T(1,128)} %bitcast.30, f32[2,128]{1,0:T(2,128)} %bitcast.29, bf16[2048,3584]{1,0:T(8,128)(2,1)} %bitcast.20, bf16[3584,2048]{1,0:T(8,128)(2,1)} %bitcast.21, bf16[4,128,3584]{2,1,0:T(8,128)(2,1)} %bitcast.22, ...), custom_call_target="tpu_custom_call" | custom-call | tf_op jit(solution)/shard_map/window/pallas_call | solution.py:489
  64.7 1.9 %copy.14 = bf16[1,128,2048]{2,1,0:T(8,128)(2,1)} copy(bf16[1,128,2048]{2,1,0:T(8,128)(2,1)} %bitcast.24) | data formatting | bytes 1048576
  66.6 1.6 %copy.15 = f32[1,4,64,128]{3,2,1,0:T(8,128)} copy(f32[1,4,64,128]{3,2,1,0:T(8,128)} %bitcast.27) | data formatting | bytes 262144

commit v2 on v1

--- a/solution.py
+++ b/solution.py
@@ -47,6 +47,8 @@
     len_ref,
     hand_out,
     feat_out,
+    hand_v,
+    feat_v,
     cot_all,
     wt_own,
     wt_all,
@@ -70,6 +72,7 @@
     trecv,
     cot_next,
     sk_sum,
+    comb,
     down_sem,
     up_sem,
     pre_sem,
@@ -95,6 +98,10 @@
     h_recv,
     k_send,
     k_recv,
+    keep_sem,
+    feat_sem,
+    c_send,
+    c_recv,
 ):
     tok, width = cot_hbm.shape
     half = tok // 2
@@ -124,7 +131,6 @@
         )
 
     own_copy = pltpu.make_async_copy(cot_hbm, cot_all.at[d], own_sem)
-    own_copy.start()
 
     def pre_copy(b, i):
         return pltpu.make_async_copy(pre_hbm.at[b], pre_v.at[b], pre_sem.at[i])
@@ -139,10 +145,7 @@
 
     for i in range(n):
         pre_copy(blocks[i], i).start()
-    for t in range(n_th):
-        down_copy(t).start()
-    for t in range(n_tn):
-        up_copy(t).start()
+    own_copy.start()
 
     block_rows = routes_ref.shape[0]
     token_block = lax.broadcasted_iota(jnp.int32, (8, tok), 1) // (tok // block_rows)
@@ -163,6 +166,12 @@
         greet += [{"section": above, "dp": blocks[i]} for i in range(n)]
     for to in greet:
         pl.semaphore_signal(barrier, inc=1, device_id=to, device_id_type=pl.DeviceIdType.MESH)
+    for i in range(n):
+        pre_copy(blocks[i], i).wait()
+    for t in range(n_th):
+        down_copy(t).start()
+    for t in range(n_tn):
+        up_copy(t).start()
     pl.semaphore_wait(barrier, len(greet))
 
     part = half // CHUNKS
@@ -179,7 +188,7 @@
     def own_line(j, to, send):
         rows = chunk(c, j)
         return remote(
-            cot_hbm.at[rows], cot_all.at[d, rows], send.at[d, j], ag_recv.at[d, j], dp=to
+            cot_all.at[d, rows], cot_all.at[d, rows], send.at[d, j], ag_recv.at[d, j], dp=to
         )
 
     def up_line(b, j):
@@ -199,7 +208,8 @@
             cot_all.at[b, rows], cot_all.at[b, rows], fw_send.at[b, j], fw_recv.at[b, j], tensor=pc
         )
 
-    cn_copy = remote(cot_hbm.at[mine_rows], cot_next, cn_send, cn_recv, section=below)
+    cn_copy = remote(cot_all.at[d, mine_rows], cot_next, cn_send, cn_recv, section=below)
+    own_copy.wait()
     for i in range(1, n):
         wt_copy(i, d).start()
 
@@ -238,7 +248,6 @@
 
                 fw_copy(d + k, j, c).start()
 
-    own_copy.wait()
     out_vec_t = lax.dot_general(
         model_ref[...], cot_all[d], NT, preferred_element_type=F32
     )
@@ -263,11 +272,25 @@
             dp=b,
         )
 
+    last = n - 1
+    is_end = (d == 0) | (d == n - 1)
+    is_inner = (d != 0) & (d != n - 1) & ((d == 1) | (d == n - 2))
+    inner = jnp.where(d == 0, 1, n - 2)
+
+    def c_copy(t):
+        return remote(osend.at[last, t], comb.at[t], c_send.at[t], c_recv.at[t], dp=inner)
+
+    def send_out(i, t):
+        if i < last:
+            o_copy(i, t, blocks[i], d).start()
+            return
+        pl.when(is_end)(lambda: c_copy(t).start())
+        if n > 4:
+            pl.when(~is_end & ~is_inner)(lambda: o_copy(i, t, blocks[i], d).start())
+
     def t_copy(i, b, source):
         return remote(tsend.at[i], trecv.at[source], t_send.at[i], t_recv.at[source], dp=b)
 
-    for i in range(n):
-        pre_copy(blocks[i], i).wait()
     down_v2[...] = jnp.zeros_like(down_v2)
 
     def ahead(t, carry):
@@ -314,16 +337,7 @@
         if arrived < n - 1:
             arrived += 1
             arrive(arrived)
-        sk_v[:, rank:] = lax.dot_general(
-            gp_v[...], sketch_ref[...], NT, preferred_element_type=F32
-        )
-        for j in range(group):
-            ssend[g, j * half : (j + 1) * half, :] = sk_v[
-                pl.ds(pl.multiple_of(j * tok + pc * half, half), half), :
-            ]
-        s_copy(g).start()
-
-        far_first = members[::-1] if g == 0 else members
+        far_first = members[::-1]
 
         def pass_on(t, g=g, members=members, far_first=far_first):
             x_copy(g, t).wait_recv()
@@ -332,7 +346,17 @@
                 j = members.index(i)
                 at = slice(j * half, (j + 1) * half)
                 osend[i, t] = (mine_v[at, cols] + xrecv[g, t, at, :].astype(F32)).astype(BF16)
-                o_copy(i, t, blocks[i], d).start()
+                send_out(i, t)
+
+        def sketch(g=g):
+            sk_v[:, rank:] = lax.dot_general(
+                gp_v[...], sketch_ref[...], NT, preferred_element_type=F32
+            )
+            for j in range(group):
+                ssend[g, j * half : (j + 1) * half, :] = sk_v[
+                    pl.ds(pl.multiple_of(j * tok + pc * half, half), half), :
+                ]
+            s_copy(g).start()
 
         def sketch_on(g=g, members=members):
             s_copy(g).wait_recv()
@@ -340,12 +364,12 @@
                 at = slice(j * half, (j + 1) * half)
                 total = sk_v[pl.ds(pl.multiple_of(j * tok + c * half, half), half), :] + srecv[g, at, :]
                 if i:
-                    tsend[i] = total
+                    tsend[i] = total.astype(BF16)
                     t_copy(i, blocks[i], d).start()
                 else:
                     sk_sum[mine_rows, :] = total
 
-        def second(t, carry, g=g, pass_on=pass_on, sketch_on=sketch_on):
+        def second(t, carry, g=g, pass_on=pass_on, sketch=sketch, sketch_on=sketch_on):
             if g == 0:
                 up_copy(t).wait()
             rows = pl.ds(pl.multiple_of(t * tn, tn), tn)
@@ -358,21 +382,32 @@
                 ].astype(BF16)
             x_copy(g, t).start()
 
+            pl.when(t == 0)(sketch)
+            pl.when(t == 1)(sketch_on)
+
             @pl.when(t > 0)
             def _():
                 pass_on(t - 1)
 
-            @pl.when(t == 1)
-            def _():
-                sketch_on()
-
             return carry
 
         lax.fori_loop(0, n_tn, second, 0)
+        need = min((g + 2) * group - 1, n - 1)
+        while g + 1 < n_groups and arrived < need:
+            arrived += 1
+            arrive(arrived)
         pass_on(n_tn - 1)
+
+    @pl.when(is_inner)
+    def _():
+        for t in range(n_tn):
+            c_copy(t).wait_recv()
+            osend[last, t] = (osend[last, t].astype(F32) + comb[t].astype(F32)).astype(BF16)
+            o_copy(last, t, blocks[last], d).start()
+
     for i in range(1, n):
         t_copy(i, blocks[i], blocks[i]).wait_recv()
-        sk_sum[mine_rows, :] += trecv[blocks[i]]
+        sk_sum[mine_rows, :] += trecv[blocks[i]].astype(F32)
 
     def k_copy(rows):
         return remote(sk_sum.at[rows], sk_sum.at[rows], k_send, k_recv, tensor=pc)
@@ -401,31 +436,55 @@
         preferred_element_type=F32,
         precision=lax.Precision.HIGHEST,
     )
-    feat_out[...] = jnp.concatenate([down_feat, up_feat], axis=1)
+    feat_v[...] = jnp.concatenate([down_feat, up_feat], axis=1)
+    feat_copy = pltpu.make_async_copy(feat_v, feat_out, feat_sem)
+    feat_copy.start()
 
     cn_copy.wait_recv()
     def h_copy(t, rows):
-        part = hand_out.at[rows, pl.ds(t * tn, tn)]
-        return remote(part, part, h_send.at[t], h_recv.at[t], tensor=pc)
+        cols = pl.ds(t * tn, tn)
+        return remote(
+            hand_v.at[rows, cols], hand_out.at[rows, cols], h_send.at[t], h_recv.at[t], tensor=pc
+        )
+
+    def keep_copy(t):
+        cols = pl.ds(t * tn, tn)
+        return pltpu.make_async_copy(
+            hand_v.at[mine_rows, cols], hand_out.at[mine_rows, cols], keep_sem.at[t]
+        )
 
     for t in range(n_tn):
         cols = slice(t * tn, (t + 1) * tn)
         total = cot_next[:, cols].astype(F32)
-        for i in range(n):
+        for i in range(last):
             o_copy(i, t, blocks[i], blocks[i]).wait_recv()
             total = total + orecv[blocks[i], t].astype(F32)
-        hand_out[mine_rows, cols] = total.astype(BF16)
+
+        @pl.when(is_end)
+        def _(total=total, cols=cols):
+            hand_v[mine_rows, cols] = total.astype(BF16)
+
+        @pl.when(~is_end)
+        def _(total=total, cols=cols, t=t):
+            o_copy(last, t, blocks[last], blocks[last]).wait_recv()
+            hand_v[mine_rows, cols] = (total + orecv[blocks[last], t].astype(F32)).astype(BF16)
+
         h_copy(t, mine_rows).start()
+        keep_copy(t).start()
 
     for t in range(n_tn):
         h_copy(t, other_rows).wait_recv()
         h_copy(t, mine_rows).wait_send()
+        keep_copy(t).wait()
+    feat_copy.wait()
     for i in range(1, n):
         wt_copy(i, d).wait_send()
         t_copy(i, blocks[i], d).wait_send()
-    for i in range(n):
-        for t in range(n_tn):
+    for t in range(n_tn):
+        for i in range(last):
             o_copy(i, t, blocks[i], d).wait_send()
+        pl.when(is_end)(lambda t=t: c_copy(t).wait_send())
+        pl.when(~is_end)(lambda t=t: o_copy(last, t, blocks[last], d).wait_send())
     for g in range(n_groups):
         s_copy(g).wait_send()
         for t in range(n_tn):
@@ -504,8 +563,10 @@
             vmem,
             pl.BlockSpec(memory_space=pltpu.SMEM),
         ],
-        out_specs=(vmem, vmem),
+        out_specs=(hbm, hbm),
         scratch_shapes=[
+            pltpu.VMEM((tok, width), BF16),
+            pltpu.VMEM((examples * rank, 2 * rank), F32),
             pltpu.VMEM((n, tok, width), BF16),
             pltpu.VMEM((n, 8, tok), F32),
             pltpu.VMEM((n, 8, tok), F32),
@@ -525,10 +586,11 @@
             pltpu.VMEM((n_g, m // 2, 2 * rank), F32),
             pltpu.VMEM((n, n_tn, half, tn), BF16),
             pltpu.VMEM((n, n_tn, half, tn), BF16),
-            pltpu.VMEM((n, half, 2 * rank), F32),
-            pltpu.VMEM((n, half, 2 * rank), F32),
+            pltpu.VMEM((n, half, 2 * rank), BF16),
+            pltpu.VMEM((n, half, 2 * rank), BF16),
             pltpu.VMEM((half, width), BF16),
             pltpu.VMEM((tok, 2 * rank), F32),
+            pltpu.VMEM((n_tn, half, tn), BF16),
             dma((n_th,)),
             dma((n_tn,)),
             dma((n,)),
@@ -554,6 +616,10 @@
             dma((n_tn,)),
             dma(()),
             dma(()),
+            dma((n_tn,)),
+            dma(()),
+            dma((n_tn,)),
+            dma((n_tn,)),
         ],
         compiler_params=pltpu.CompilerParams(
             collective_id=0, has_side_effects=True, vmem_limit_bytes=63 * 1024 * 1024

time: 68.4 us -> 61.9 us (0.905)
  Pallas kernels: 64.1 us -> 57.6 us
    pallas_call x1, Pallas kernels: 64.1 us -> 57.6 us  [per_device(): pl.pallas_call(functools.partial(kernel, n, sections, group, th, tn), out...]
where the time goes in v2:
time: 61.9 us; the launch traced here: 61.7 us
  Pallas kernels  57.6 us (93%)
  local copies, waits for them, and re-layouts  3.45 us (6%)
  between operations  0.64 us (1%)
    pallas_call x1, Pallas kernels, per_device(): pl.pallas_call(functools.partial(kernel, n, sections, group, th, tn), out...  57.6 us
    unnamed x2, local copies, waits for them, and re-layouts  3.45 us

profile of v2, /device:TPU:0, one launch (start us, length us, event | category | flops | bytes accessed | tf_op | source)
XLA Modules:
  0.0 61.7 jit_solution(7864467318807186365)
XLA Ops:
  0.6 57.6 %window.1 = (bf16[128,2048]{1,0:T(8,128)(2,1)}, f32[256,128]{1,0:T(8,128)}) custom-call(bf16[128,2048]{1,0:T(8,128)(2,1)} %bitcast.23, s32[1,2]{1,0:T(1,128)} %bitcast.30, f32[2,128]{1,0:T(2,128)} %bitcast.29, bf16[2048,3584]{1,0:T(8,128)(2,1)} %bitcast.20, bf16[3584,2048]{1,0:T(8,128)(2,1)} %bitcast.21, bf16[4,128,3584]{2,1,0:T(8,128)(2,1)} %bitcast.22, ...), custom_call_target="tpu_custom_call" | custom-call | tf_op jit(solution)/shard_map/window/pallas_call | solution.py:548
  58.2 1.9 %copy.14 = bf16[1,128,2048]{2,1,0:T(8,128)(2,1)} copy(bf16[1,128,2048]{2,1,0:T(8,128)(2,1)} %bitcast.24) | data formatting | bytes 1048576
  60.1 1.6 %copy.15 = f32[1,4,64,128]{3,2,1,0:T(8,128)} copy(f32[1,4,64,128]{3,2,1,0:T(8,128)} %bitcast.27) | data formatting | bytes 262144

commit v3 on v2

--- a/solution.py
+++ b/solution.py
@@ -225,28 +225,32 @@
 
     cn_copy.start()
 
-    def arrive(k, chunks=range(CHUNKS)):
-        for j in chunks:
-
-            @pl.when(d >= k)
-            def _(j=j):
-                up_line(d - k, j).wait_recv()
-
-                @pl.when(d < n - 1)
-                def _():
-                    up_line(d - k, j).start()
-
-                fw_copy(d - k, j, c).start()
-
-            @pl.when(d + k < n)
-            def _(j=j):
-                down_line(d + k, j).wait_recv()
-
-                @pl.when(d > 0)
-                def _():
-                    down_line(d + k, j).start()
-
-                fw_copy(d + k, j, c).start()
+    is_upper = d >= n // 2
+
+    def arrive(k):
+        def take(b, line, may, at_once):
+            def pass_chunk(j):
+                pl.when(may)(lambda: line(b, j).start())
+
+            def pass_all():
+                for j in range(CHUNKS):
+                    pass_chunk(j)
+
+            for j in range(CHUNKS):
+                line(b, j).wait_recv()
+                pl.when(at_once)(lambda j=j: pass_chunk(j))
+                fw_copy(b, j, c).start()
+            pl.when(~at_once)(pass_all)
+
+        def from_low():
+            take(d - k, up_line, d < n - 1, ~is_upper | (k > 1))
+
+        def from_high():
+            take(d + k, down_line, d > 0, is_upper | (k > 1))
+
+        pl.when(is_upper & (d >= k))(from_low)
+        pl.when(d + k < n)(from_high)
+        pl.when(~is_upper & (d >= k))(from_low)
 
     out_vec_t = lax.dot_general(
         model_ref[...], cot_all[d], NT, preferred_element_type=F32
@@ -382,10 +386,14 @@
                 ].astype(BF16)
             x_copy(g, t).start()
 
-            pl.when(t == 0)(sketch)
+            @pl.when(t == 0)
+            def _():
+                sketch()
+                pass_on(0)
+
             pl.when(t == 1)(sketch_on)
 
-            @pl.when(t > 0)
+            @pl.when(t > 1)
             def _():
                 pass_on(t - 1)
 
@@ -396,7 +404,8 @@
         while g + 1 < n_groups and arrived < need:
             arrived += 1
             arrive(arrived)
-        pass_on(n_tn - 1)
+        if n_tn > 1:
+            pass_on(n_tn - 1)
 
     @pl.when(is_inner)
     def _():
@@ -514,7 +523,25 @@
     k_copy(mine_rows).wait_send()
 
 
+def hand_over(parts, hand_in, feat_in, hand_out, feat_out, hand_v, feat_v, in_sem, out_sem):
+    rows = hand_in.shape[0] // parts
+    into = [pltpu.make_async_copy(feat_in, feat_v, in_sem.at[parts])]
+    out = [pltpu.make_async_copy(feat_v, feat_out, out_sem.at[parts])]
+    for j in range(parts):
+        at = pl.ds(j * rows, rows)
+        into.append(pltpu.make_async_copy(hand_in.at[at], hand_v.at[at], in_sem.at[j]))
+        out.append(pltpu.make_async_copy(hand_v.at[at], hand_out.at[at], out_sem.at[j]))
+    for copy in into:
+        copy.start()
+    for copy, then in zip(into, out):
+        copy.wait()
+        then.start()
+    for copy in out:
+        copy.wait()
+
+
 GROUP = 2
+PARTS = 2
 CHUNKS = 2
 
 
@@ -637,6 +664,22 @@
         hidden_sketch[0, 0].T,
         lengths[0, 0],
     )
+    hand, feat = pl.pallas_call(
+        functools.partial(hand_over, PARTS),
+        out_shape=(
+            jax.ShapeDtypeStruct(hand.shape, BF16),
+            jax.ShapeDtypeStruct(feat.shape, F32),
+        ),
+        in_specs=[hbm, hbm],
+        out_specs=(hbm, hbm),
+        scratch_shapes=[
+            pltpu.VMEM(hand.shape, BF16),
+            pltpu.VMEM(feat.shape, F32),
+            dma((PARTS + 1,)),
+            dma((PARTS + 1,)),
+        ],
+        name="hand_over",
+    )(hand, feat)
     return (hand[None], feat.reshape(1, examples, rank, 2 * rank))
 
 

time: 61.9 us -> 58.9 us (0.952)
  local copies, waits for them, and re-layouts: 3.45 us -> 0 us
    unnamed x2 -> x0, local copies, waits for them, and re-layouts: 3.45 us -> none
    pallas_call x0 -> x1, Pallas kernels: none -> 1.86 us  [per_device(): pl.pallas_call(functools.partial(hand_over, PARTS), out_shape=(jax.ShapeD...]
    pallas_call x1, Pallas kernels: 57.6 us -> 56.2 us  [per_device(): pl.pallas_call(functools.partial(kernel, n, sections, group, th, tn), out...]
where the time goes in v3:
time: 58.9 us; the launch traced here: 58.7 us
  Pallas kernels  58.1 us (99%)
  between operations  0.64 us (1%)
    pallas_call x1, Pallas kernels, per_device(): pl.pallas_call(functools.partial(kernel, n, sections, group, th, tn), out...  56.2 us
    pallas_call x1, Pallas kernels, per_device(): pl.pallas_call(functools.partial(hand_over, PARTS), out_shape=(jax.ShapeD...  1.86 us

profile of v3, /device:TPU:0, one launch (start us, length us, event | category | flops | bytes accessed | tf_op | source)
XLA Modules:
  0.0 58.7 jit_solution(11792114595141986619)
XLA Ops:
  0.6 56.2 %window.1 = (bf16[128,2048]{1,0:T(8,128)(2,1)}, f32[256,128]{1,0:T(8,128)}) custom-call(bf16[128,2048]{1,0:T(8,128)(2,1)} %bitcast.23, s32[1,2]{1,0:T(1,128)} %bitcast.28, f32[2,128]{1,0:T(2,128)} %bitcast.27, bf16[2048,3584]{1,0:T(8,128)(2,1)} %bitcast.20, bf16[3584,2048]{1,0:T(8,128)(2,1)} %bitcast.21, bf16[4,128,3584]{2,1,0:T(8,128)(2,1)} %bitcast.22, ...), custom_call_target="tpu_custom_call" | custom-call | tf_op jit(solution)/shard_map/window/pallas_call | solution.py:575
  56.9 1.9 %hand_over.1 = (bf16[128,2048]{1,0:T(8,128)(2,1)}, f32[256,128]{1,0:T(8,128)}) custom-call(bf16[128,2048]{1,0:T(8,128)(2,1)} %get-tuple-element.6.hand_in, f32[256,128]{1,0:T(8,128)} %get-tuple-element.7.feat_in), custom_call_target="tpu_custom_call" | custom-call | tf_op jit(solution)/shard_map/hand_over/pallas_call | solution.py:667

commit v4 on v3

--- a/solution.py
+++ b/solution.py
@@ -100,7 +100,6 @@
     k_recv,
     keep_sem,
     feat_sem,
-    c_send,
     c_recv,
 ):
     tok, width = cot_hbm.shape
@@ -133,7 +132,7 @@
     own_copy = pltpu.make_async_copy(cot_hbm, cot_all.at[d], own_sem)
 
     def pre_copy(b, i):
-        return pltpu.make_async_copy(pre_hbm.at[b], pre_v.at[b], pre_sem.at[i])
+        return pltpu.make_async_copy(pre_hbm.at[b], pre_v.at[b], pre_sem)
 
     def down_copy(t):
         rows = pl.ds(pl.multiple_of(t * th, th), th)
@@ -166,64 +165,63 @@
         greet += [{"section": above, "dp": blocks[i]} for i in range(n)]
     for to in greet:
         pl.semaphore_signal(barrier, inc=1, device_id=to, device_id_type=pl.DeviceIdType.MESH)
-    for i in range(n):
-        pre_copy(blocks[i], i).wait()
+    pl.semaphore_wait(barrier, len(greet))
+
+    part = half // CHUNKS
+
+    def chunk(core, j):
+        return pl.ds(pl.multiple_of(core * half + j * part, part), part)
+
+    def line_copy(b, j, to, send):
+        rows = chunk(c, j)
+        return remote(
+            cot_all.at[b, rows], cot_all.at[b, rows], send, ag_recv.at[b, j], dp=to
+        )
+
+    def own_line(j, to, send):
+        rows = chunk(c, j)
+        return remote(
+            cot_hbm.at[rows], cot_all.at[d, rows], send, ag_recv.at[d, j], dp=to
+        )
+
+    def up_line(b, j):
+        return line_copy(b, j, jnp.minimum(d + 1, n - 1), up_send)
+
+    def down_line(b, j):
+        return line_copy(b, j, jnp.maximum(d - 1, 0), dn_send)
+
+    def wt_copy(i, source):
+        return remote(
+            wt_own.at[blocks[i]], wt_all.at[source], wt_send, wt_recv.at[source], dp=blocks[i]
+        )
+
+    def fw_copy(b, j, core):
+        rows = chunk(core, j)
+        return remote(
+            cot_all.at[b, rows], cot_all.at[b, rows], fw_send, fw_recv.at[b, j], tensor=pc
+        )
+
+    cn_copy = remote(cot_hbm.at[mine_rows], cot_next, cn_send, cn_recv, section=below)
+    for i in range(1, n):
+        wt_copy(i, d).start()
+
+    @pl.when(d < n - 1)
+    def _():
+        for j in range(CHUNKS):
+            own_line(j, d + 1, up_send).start()
+
+    @pl.when(d > 0)
+    def _():
+        for j in range(CHUNKS):
+            own_line(j, d - 1, dn_send).start()
+
+    cn_copy.start()
+    pltpu.make_async_copy(pre_hbm, pre_v, pre_sem).wait()
     for t in range(n_th):
         down_copy(t).start()
     for t in range(n_tn):
         up_copy(t).start()
-    pl.semaphore_wait(barrier, len(greet))
-
-    part = half // CHUNKS
-
-    def chunk(core, j):
-        return pl.ds(pl.multiple_of(core * half + j * part, part), part)
-
-    def line_copy(b, j, to, send):
-        rows = chunk(c, j)
-        return remote(
-            cot_all.at[b, rows], cot_all.at[b, rows], send.at[b, j], ag_recv.at[b, j], dp=to
-        )
-
-    def own_line(j, to, send):
-        rows = chunk(c, j)
-        return remote(
-            cot_all.at[d, rows], cot_all.at[d, rows], send.at[d, j], ag_recv.at[d, j], dp=to
-        )
-
-    def up_line(b, j):
-        return line_copy(b, j, jnp.minimum(d + 1, n - 1), up_send)
-
-    def down_line(b, j):
-        return line_copy(b, j, jnp.maximum(d - 1, 0), dn_send)
-
-    def wt_copy(i, source):
-        return remote(
-            wt_own.at[blocks[i]], wt_all.at[source], wt_send.at[i], wt_recv.at[source], dp=blocks[i]
-        )
-
-    def fw_copy(b, j, core):
-        rows = chunk(core, j)
-        return remote(
-            cot_all.at[b, rows], cot_all.at[b, rows], fw_send.at[b, j], fw_recv.at[b, j], tensor=pc
-        )
-
-    cn_copy = remote(cot_all.at[d, mine_rows], cot_next, cn_send, cn_recv, section=below)
     own_copy.wait()
-    for i in range(1, n):
-        wt_copy(i, d).start()
-
-    @pl.when(d < n - 1)
-    def _():
-        for j in range(CHUNKS):
-            own_line(j, d + 1, up_send).start()
-
-    @pl.when(d > 0)
-    def _():
-        for j in range(CHUNKS):
-            own_line(j, d - 1, dn_send).start()
-
-    cn_copy.start()
 
     is_upper = d >= n // 2
 
@@ -261,17 +259,17 @@
     )
 
     def x_copy(g, t):
-        return remote(xsend.at[g, t], xrecv.at[g, t], x_send.at[g, t], x_recv.at[g, t], tensor=pc)
+        return remote(xsend.at[g, t], xrecv.at[g, t], x_send, x_recv.at[g, t], tensor=pc)
 
     def s_copy(g):
-        return remote(ssend.at[g], srecv.at[g], s_send.at[g], s_recv.at[g], tensor=pc)
+        return remote(ssend.at[g], srecv.at[g], s_send, s_recv.at[g], tensor=pc)
 
     def o_copy(i, t, b, source):
         return remote(
             osend.at[i, t],
-            orecv.at[source, t],
-            o_send.at[i, t],
-            o_recv.at[source, t],
+            orecv.at[t, source],
+            o_send,
+            o_recv.at[t],
             section=below,
             dp=b,
         )
@@ -281,19 +279,40 @@
     is_inner = (d != 0) & (d != n - 1) & ((d == 1) | (d == n - 2))
     inner = jnp.where(d == 0, 1, n - 2)
 
-    def c_copy(t):
-        return remote(osend.at[last, t], comb.at[t], c_send.at[t], c_recv.at[t], dp=inner)
+    piece = half // SPLIT
+
+    def c_copy(t, k):
+        rows = pl.ds(k * piece, piece)
+        return remote(
+            osend.at[last, t, rows], comb.at[t, rows], o_send, c_recv.at[t, k], dp=inner
+        )
+
+    def c_start(t):
+        for k in range(SPLIT):
+            c_copy(t, k).start()
+
+    def c_onward(t, k):
+        rows = pl.ds(k * piece, piece)
+        b = blocks[last]
+        return remote(
+            osend.at[last, t, rows],
+            orecv.at[t, d, rows],
+            o_send,
+            o_recv.at[t],
+            section=below,
+            dp=b,
+        )
 
     def send_out(i, t):
         if i < last:
             o_copy(i, t, blocks[i], d).start()
             return
-        pl.when(is_end)(lambda: c_copy(t).start())
+        pl.when(is_end)(lambda: c_start(t))
         if n > 4:
             pl.when(~is_end & ~is_inner)(lambda: o_copy(i, t, blocks[i], d).start())
 
     def t_copy(i, b, source):
-        return remote(tsend.at[i], trecv.at[source], t_send.at[i], t_recv.at[source], dp=b)
+        return remote(tsend.at[i], trecv.at[source], t_send, t_recv, dp=b)
 
     down_v2[...] = jnp.zeros_like(down_v2)
 
@@ -410,12 +429,17 @@
     @pl.when(is_inner)
     def _():
         for t in range(n_tn):
-            c_copy(t).wait_recv()
-            osend[last, t] = (osend[last, t].astype(F32) + comb[t].astype(F32)).astype(BF16)
-            o_copy(last, t, blocks[last], d).start()
-
+            for k in range(SPLIT):
+                rows = slice(k * piece, (k + 1) * piece)
+                c_copy(t, k).wait_recv()
+                osend[last, t, rows] = (
+                    osend[last, t, rows].astype(F32) + comb[t, rows].astype(F32)
+                ).astype(BF16)
+                c_onward(t, k).start()
+
+    parts = pl.ds(0, n - 1)
+    remote(tsend.at[parts], trecv.at[parts], t_send, t_recv, dp=blocks[1]).wait_recv()
     for i in range(1, n):
-        t_copy(i, blocks[i], blocks[i]).wait_recv()
         sk_sum[mine_rows, :] += trecv[blocks[i]].astype(F32)
 
     def k_copy(rows):
@@ -453,21 +477,27 @@
     def h_copy(t, rows):
         cols = pl.ds(t * tn, tn)
         return remote(
-            hand_v.at[rows, cols], hand_out.at[rows, cols], h_send.at[t], h_recv.at[t], tensor=pc
+            hand_v.at[rows, cols], hand_out.at[rows, cols], h_send, h_recv, tensor=pc
         )
 
     def keep_copy(t):
         cols = pl.ds(t * tn, tn)
         return pltpu.make_async_copy(
-            hand_v.at[mine_rows, cols], hand_out.at[mine_rows, cols], keep_sem.at[t]
+            hand_v.at[mine_rows, cols], hand_out.at[mine_rows, cols], keep_sem
         )
 
     for t in range(n_tn):
         cols = slice(t * tn, (t + 1) * tn)
+
+        def landed(count, t=t):
+            box = orecv.at[t, pl.ds(0, count)]
+            remote(box, box, o_send, o_recv.at[t], section=below).wait_recv()
+
+        pl.when(is_end)(functools.partial(landed, n - 1))
+        pl.when(~is_end)(functools.partial(landed, n))
         total = cot_next[:, cols].astype(F32)
         for i in range(last):
-            o_copy(i, t, blocks[i], blocks[i]).wait_recv()
-            total = total + orecv[blocks[i], t].astype(F32)
+            total = total + orecv[t, blocks[i]].astype(F32)
 
         @pl.when(is_end)
         def _(total=total, cols=cols):
@@ -475,50 +505,29 @@
 
         @pl.when(~is_end)
         def _(total=total, cols=cols, t=t):
-            o_copy(last, t, blocks[last], blocks[last]).wait_recv()
-            hand_v[mine_rows, cols] = (total + orecv[blocks[last], t].astype(F32)).astype(BF16)
+            hand_v[mine_rows, cols] = (total + orecv[t, blocks[last]].astype(F32)).astype(BF16)
 
         h_copy(t, mine_rows).start()
         keep_copy(t).start()
 
-    for t in range(n_tn):
-        h_copy(t, other_rows).wait_recv()
-        h_copy(t, mine_rows).wait_send()
-        keep_copy(t).wait()
+    remote(hand_v.at[other_rows], hand_out.at[other_rows], h_send, h_recv, tensor=pc).wait_recv()
+    remote(hand_v.at[mine_rows], hand_out.at[mine_rows], h_send, h_recv, tensor=pc).wait_send()
+    pltpu.make_async_copy(hand_v.at[mine_rows], hand_out.at[mine_rows], keep_sem).wait()
     feat_copy.wait()
-    for i in range(1, n):
-        wt_copy(i, d).wait_send()
-        t_copy(i, blocks[i], d).wait_send()
-    for t in range(n_tn):
-        for i in range(last):
-            o_copy(i, t, blocks[i], d).wait_send()
-        pl.when(is_end)(lambda t=t: c_copy(t).wait_send())
-        pl.when(~is_end)(lambda t=t: o_copy(last, t, blocks[last], d).wait_send())
-    for g in range(n_groups):
-        s_copy(g).wait_send()
-        for t in range(n_tn):
-            x_copy(g, t).wait_send()
-    for k in range(n):
-        for j in range(CHUNKS):
-
-            @pl.when(d >= k)
-            def _(k=k, j=j):
-                @pl.when(d < n - 1)
-                def _():
-                    up_line(d - k, j).wait_send()
-
-                if k:
-                    fw_copy(d - k, j, c).wait_send()
-
-            @pl.when(d + k < n)
-            def _(k=k, j=j):
-                @pl.when(d > 0)
-                def _():
-                    down_line(d + k, j).wait_send()
-
-                if k:
-                    fw_copy(d + k, j, c).wait_send()
-
+
+    def drain(ref, sem):
+        remote(ref, ref, sem, sem, tensor=pc).wait_send()
+
+    drain(wt_own.at[parts], wt_send)
+    drain(tsend.at[parts], t_send)
+    drain(osend, o_send)
+    drain(ssend, s_send)
+    drain(xsend, x_send)
+    drain(cot_all.at[parts, pl.ds(0, half)], fw_send)
+    for m in range(1, n):
+        rows = cot_all.at[pl.ds(0, m), pl.ds(0, half)]
+        pl.when(d == m - 1)(functools.partial(drain, rows, up_send))
+        pl.when(d == n - m)(functools.partial(drain, rows, dn_send))
     cn_copy.wait_send()
     k_copy(mine_rows).wait_send()
 
@@ -541,7 +550,8 @@
 
 
 GROUP = 2
-PARTS = 2
+SPLIT = 1
+PARTS = 1
 CHUNKS = 2
 
 
@@ -612,7 +622,7 @@
             pltpu.VMEM((n_g, m // 2, 2 * rank), F32),
             pltpu.VMEM((n_g, m // 2, 2 * rank), F32),
             pltpu.VMEM((n, n_tn, half, tn), BF16),
-            pltpu.VMEM((n, n_tn, half, tn), BF16),
+            pltpu.VMEM((n_tn, n, half, tn), BF16),
             pltpu.VMEM((n, half, 2 * rank), BF16),
             pltpu.VMEM((n, half, 2 * rank), BF16),
             pltpu.VMEM((half, width), BF16),
@@ -620,33 +630,32 @@
             pltpu.VMEM((n_tn, half, tn), BF16),
             dma((n_th,)),
             dma((n_tn,)),
+            dma(()),
+            dma(()),
+            dma(()),
+            dma(()),
+            dma((n, CHUNKS)),
+            dma(()),
             dma((n,)),
             dma(()),
             dma((n, CHUNKS)),
-            dma((n, CHUNKS)),
-            dma((n, CHUNKS)),
-            dma((n,)),
-            dma((n,)),
-            dma((n, CHUNKS)),
-            dma((n, CHUNKS)),
+            dma(()),
             dma(()),
             dma(()),
             dma((n_g, n_tn)),
-            dma((n_g, n_tn)),
+            dma(()),
             dma((n_g,)),
-            dma((n_g,)),
-            dma((n, n_tn)),
-            dma((n, n_tn)),
-            dma((n,)),
-            dma((n,)),
+            dma(()),
             dma((n_tn,)),
-            dma((n_tn,)),
-            dma(()),
-            dma(()),
-            dma((n_tn,)),
-            dma(()),
-            dma((n_tn,)),
-            dma((n_tn,)),
+            dma(()),
+            dma(()),
+            dma(()),
+            dma(()),
+            dma(()),
+            dma(()),
+            dma(()),
+            dma(()),
+            dma((n_tn, SPLIT)),
         ],
         compiler_params=pltpu.CompilerParams(
             collective_id=0, has_side_effects=True, vmem_limit_bytes=63 * 1024 * 1024

time: 58.9 us -> 57.4 us (0.975)
  Pallas kernels: 58.1 us -> 56.6 us
    pallas_call x1, Pallas kernels: 56.2 us -> 54.7 us  [per_device(): pl.pallas_call(functools.partial(kernel, n, sections, group, th, tn), out...]
where the time goes in v4:
time: 57.4 us; the launch traced here: 57.3 us
  Pallas kernels  56.6 us (99%)
  between operations  0.64 us (1%)
    pallas_call x1, Pallas kernels, per_device(): pl.pallas_call(functools.partial(kernel, n, sections, group, th, tn), out...  54.7 us
    pallas_call x1, Pallas kernels, per_device(): pl.pallas_call(functools.partial(hand_over, PARTS), out_shape=(jax.ShapeD...  1.94 us

profile of v4, /device:TPU:0, one launch (start us, length us, event | category | flops | bytes accessed | tf_op | source)
XLA Modules:
  0.0 57.3 jit_solution(5310479306518080695)
XLA Ops:
  0.6 54.7 %window.1 = (bf16[128,2048]{1,0:T(8,128)(2,1)}, f32[256,128]{1,0:T(8,128)}) custom-call(bf16[128,2048]{1,0:T(8,128)(2,1)} %bitcast.23, s32[1,2]{1,0:T(1,128)} %bitcast.28, f32[2,128]{1,0:T(2,128)} %bitcast.27, bf16[2048,3584]{1,0:T(8,128)(2,1)} %bitcast.20, bf16[3584,2048]{1,0:T(8,128)(2,1)} %bitcast.21, bf16[4,128,3584]{2,1,0:T(8,128)(2,1)} %bitcast.22, ...), custom_call_target="tpu_custom_call" | custom-call | tf_op jit(solution)/shard_map/window/pallas_call | solution.py:585
  55.3 1.9 %hand_over.1 = (bf16[128,2048]{1,0:T(8,128)(2,1)}, f32[256,128]{1,0:T(8,128)}) custom-call(bf16[128,2048]{1,0:T(8,128)(2,1)} %get-tuple-element.6.hand_in, f32[256,128]{1,0:T(8,128)} %get-tuple-element.7.feat_in), custom_call_target="tpu_custom_call" | custom-call | tf_op jit(solution)/shard_map/hand_over/pallas_call | solution.py:676

commit v5 on v4

--- a/solution.py
+++ b/solution.py
@@ -36,15 +36,15 @@
     th,
     tn,
     cot_hbm,
-    routes_ref,
-    gates_ref,
+    routes_hbm,
+    gates_hbm,
     up_hbm,
     down_hbm,
     pre_hbm,
-    insk_ref,
-    model_ref,
-    sketch_ref,
-    len_ref,
+    insk_hbm,
+    model_hbm,
+    sketch_hbm,
+    len_hbm,
     hand_out,
     feat_out,
     hand_v,
@@ -101,11 +101,18 @@
     keep_sem,
     feat_sem,
     c_recv,
+    routes_ref,
+    gates_ref,
+    insk_ref,
+    model_ref,
+    sketch_ref,
+    len_ref,
+    small_sem,
 ):
     tok, width = cot_hbm.shape
     half = tok // 2
     hidden_cols = up_hbm.shape[1]
-    rank = insk_ref.shape[0]
+    rank = insk_hbm.shape[0]
     d = lax.axis_index("dp")
     s = lax.axis_index("section")
     c = lax.axis_index("tensor")
@@ -129,6 +136,27 @@
             device_id_type=pl.DeviceIdType.MESH,
         )
 
+    barrier = pltpu.get_barrier_semaphore()
+    greet = [{"tensor": pc}]
+    greet += [{"dp": blocks[i]} for i in range(1, n)]
+    greet += [{"section": below, "dp": blocks[i]} for i in range(n)]
+    if sections > 2:
+        greet += [{"section": above, "dp": blocks[i]} for i in range(n)]
+    for to in greet:
+        pl.semaphore_signal(barrier, inc=1, device_id=to, device_id_type=pl.DeviceIdType.MESH)
+    small = [
+        pltpu.make_async_copy(source, kept, small_sem.at[i])
+        for i, (source, kept) in enumerate(
+            (
+                (routes_hbm, routes_ref),
+                (gates_hbm, gates_ref),
+                (sketch_hbm, sketch_ref),
+                (model_hbm, model_ref),
+                (insk_hbm, insk_ref),
+                (len_hbm, len_ref),
+            )
+        )
+    ]
     own_copy = pltpu.make_async_copy(cot_hbm, cot_all.at[d], own_sem)
 
     def pre_copy(b, i):
@@ -145,7 +173,65 @@
     for i in range(n):
         pre_copy(blocks[i], i).start()
     own_copy.start()
-
+    for copy in small:
+        copy.start()
+
+    pl.semaphore_wait(barrier, len(greet))
+
+    part = half // CHUNKS
+
+    def chunk(core, j):
+        return pl.ds(pl.multiple_of(core * half + j * part, part), part)
+
+    def line_copy(b, j, to, send):
+        rows = chunk(c, j)
+        return remote(
+            cot_all.at[b, rows], cot_all.at[b, rows], send, ag_recv.at[b, j], dp=to
+        )
+
+    def own_line(j, to, send):
+        rows = chunk(c, j)
+        return remote(
+            cot_hbm.at[rows], cot_all.at[d, rows], send, ag_recv.at[d, j], dp=to
+        )
+
+    def up_line(b, j):
+        return line_copy(b, j, jnp.minimum(d + 1, n - 1), up_send)
+
+    def down_line(b, j):
+        return line_copy(b, j, jnp.maximum(d - 1, 0), dn_send)
+
+    def wt_copy(i, source):
+        return remote(
+            wt_own.at[blocks[i]], wt_all.at[source], wt_send, wt_recv.at[source], dp=blocks[i]
+        )
+
+    def fw_copy(b, j, core):
+        rows = chunk(core, j)
+        return remote(
+            cot_all.at[b, rows], cot_all.at[b, rows], fw_send, fw_recv.at[b, j], tensor=pc
+        )
+
+    cn_copy = remote(cot_hbm.at[mine_rows], cot_next, cn_send, cn_recv, section=below)
+
+    @pl.when(d < n - 1)
+    def _():
+        for j in range(CHUNKS):
+            own_line(j, d + 1, up_send).start()
+
+    @pl.when(d > 0)
+    def _():
+        for j in range(CHUNKS):
+            own_line(j, d - 1, dn_send).start()
+
+    cn_copy.start()
+    pltpu.make_async_copy(pre_hbm, pre_v, pre_sem).wait()
+    for t in range(n_th):
+        down_copy(t).start()
+    for t in range(n_tn):
+        up_copy(t).start()
+    for copy in small:
+        copy.wait()
     block_rows = routes_ref.shape[0]
     token_block = lax.broadcasted_iota(jnp.int32, (8, tok), 1) // (tok // block_rows)
     for p in range(n):
@@ -157,70 +243,8 @@
                 weight += jnp.where(routes_ref[q, k] == expert, share, 0.0)
         wt_own[p] = weight
 
-    barrier = pltpu.get_barrier_semaphore()
-    greet = [{"tensor": pc}]
-    greet += [{"dp": blocks[i]} for i in range(1, n)]
-    greet += [{"section": below, "dp": blocks[i]} for i in range(n)]
-    if sections > 2:
-        greet += [{"section": above, "dp": blocks[i]} for i in range(n)]
-    for to in greet:
-        pl.semaphore_signal(barrier, inc=1, device_id=to, device_id_type=pl.DeviceIdType.MESH)
-    pl.semaphore_wait(barrier, len(greet))
-
-    part = half // CHUNKS
-
-    def chunk(core, j):
-        return pl.ds(pl.multiple_of(core * half + j * part, part), part)
-
-    def line_copy(b, j, to, send):
-        rows = chunk(c, j)
-        return remote(
-            cot_all.at[b, rows], cot_all.at[b, rows], send, ag_recv.at[b, j], dp=to
-        )
-
-    def own_line(j, to, send):
-        rows = chunk(c, j)
-        return remote(
-            cot_hbm.at[rows], cot_all.at[d, rows], send, ag_recv.at[d, j], dp=to
-        )
-
-    def up_line(b, j):
-        return line_copy(b, j, jnp.minimum(d + 1, n - 1), up_send)
-
-    def down_line(b, j):
-        return line_copy(b, j, jnp.maximum(d - 1, 0), dn_send)
-
-    def wt_copy(i, source):
-        return remote(
-            wt_own.at[blocks[i]], wt_all.at[source], wt_send, wt_recv.at[source], dp=blocks[i]
-        )
-
-    def fw_copy(b, j, core):
-        rows = chunk(core, j)
-        return remote(
-            cot_all.at[b, rows], cot_all.at[b, rows], fw_send, fw_recv.at[b, j], tensor=pc
-        )
-
-    cn_copy = remote(cot_hbm.at[mine_rows], cot_next, cn_send, cn_recv, section=below)
     for i in range(1, n):
         wt_copy(i, d).start()
-
-    @pl.when(d < n - 1)
-    def _():
-        for j in range(CHUNKS):
-            own_line(j, d + 1, up_send).start()
-
-    @pl.when(d > 0)
-    def _():
-        for j in range(CHUNKS):
-            own_line(j, d - 1, dn_send).start()
-
-    cn_copy.start()
-    pltpu.make_async_copy(pre_hbm, pre_v, pre_sem).wait()
-    for t in range(n_th):
-        down_copy(t).start()
-    for t in range(n_tn):
-        up_copy(t).start()
     own_copy.wait()
 
     is_upper = d >= n // 2
@@ -580,7 +604,6 @@
     tn = tile_of(width, 512)
     n_th, n_tn, n_g = hidden_cols // th, width // tn, n // group
     dma = pltpu.SemaphoreType.DMA
-    vmem = pl.BlockSpec(memory_space=pltpu.VMEM)
     hbm = pl.BlockSpec(memory_space=pl.ANY)
     hand, feat = pl.pallas_call(
         functools.partial(kernel, n, sections, group, th, tn),
@@ -588,18 +611,7 @@
             jax.ShapeDtypeStruct((tok, width), BF16),
             jax.ShapeDtypeStruct((examples * rank, 2 * rank), F32),
         ),
-        in_specs=[
-            hbm,
-            pl.BlockSpec(memory_space=pltpu.SMEM),
-            vmem,
-            hbm,
-            hbm,
-            hbm,
-            vmem,
-            vmem,
-            vmem,
-            pl.BlockSpec(memory_space=pltpu.SMEM),
-        ],
+        in_specs=[hbm] * 10,
         out_specs=(hbm, hbm),
         scratch_shapes=[
             pltpu.VMEM((tok, width), BF16),
@@ -656,6 +668,13 @@
             dma(()),
             dma(()),
             dma((n_tn, SPLIT)),
+            pltpu.SMEM(routes.shape[1:], jnp.int32),
+            pltpu.VMEM((2, tok), F32),
+            pltpu.VMEM((rank, tok), F32),
+            pltpu.VMEM((rank, width), BF16),
+            pltpu.VMEM((rank, hidden_cols), BF16),
+            pltpu.SMEM((examples,), jnp.int32),
+            dma((6,)),
         ],
         compiler_params=pltpu.CompilerParams(
             collective_id=0, has_side_effects=True, vmem_limit_bytes=63 * 1024 * 1024

time: 57.4 us -> 56.2 us (0.979)
  Pallas kernels: 56.6 us -> 55.4 us
    pallas_call x1, Pallas kernels: 54.7 us -> 53.5 us  [per_device(): pl.pallas_call(functools.partial(kernel, n, sections, group, th, tn), out...]
where the time goes in v5:
time: 56.2 us; the launch traced here: 56.1 us
  Pallas kernels  55.4 us (99%)
  between operations  0.64 us (1%)
    pallas_call x1, Pallas kernels, per_device(): pl.pallas_call(functools.partial(kernel, n, sections, group, th, tn), out...  53.5 us
    pallas_call x1, Pallas kernels, per_device(): pl.pallas_call(functools.partial(hand_over, PARTS), out_shape=(jax.ShapeD...  1.94 us

profile of v5, /device:TPU:0, one launch (start us, length us, event | category | flops | bytes accessed | tf_op | source)
XLA Modules:
  0.0 56.1 jit_solution(11728090235946803574)
XLA Ops:
  0.6 53.5 %window.1 = (bf16[128,2048]{1,0:T(8,128)(2,1)}, f32[256,128]{1,0:T(8,128)}) custom-call(bf16[128,2048]{1,0:T(8,128)(2,1)} %bitcast.23, s32[1,2]{1,0:T(1,128)} %bitcast.28, f32[2,128]{1,0:T(2,128)} %bitcast.27, bf16[2048,3584]{1,0:T(8,128)(2,1)} %bitcast.20, bf16[3584,2048]{1,0:T(8,128)(2,1)} %bitcast.21, bf16[4,128,3584]{2,1,0:T(8,128)(2,1)} %bitcast.22, ...), custom_call_target="tpu_custom_call" | custom-call | tf_op jit(solution)/shard_map/window/pallas_call | solution.py:608
  54.1 1.9 %hand_over.1 = (bf16[128,2048]{1,0:T(8,128)(2,1)}, f32[256,128]{1,0:T(8,128)}) custom-call(bf16[128,2048]{1,0:T(8,128)(2,1)} %get-tuple-element.6.hand_in, f32[256,128]{1,0:T(8,128)} %get-tuple-element.7.feat_in), custom_call_target="tpu_custom_call" | custom-call | tf_op jit(solution)/shard_map/hand_over/pallas_call | solution.py:695

commit v6 on v5

--- a/solution.py
+++ b/solution.py
@@ -100,6 +100,9 @@
     k_recv,
     keep_sem,
     feat_sem,
+    low_in,
+    high_in,
+    line_in,
     c_recv,
     routes_ref,
     gates_ref,
@@ -137,13 +140,17 @@
         )
 
     barrier = pltpu.get_barrier_semaphore()
-    greet = [{"tensor": pc}]
-    greet += [{"dp": blocks[i]} for i in range(1, n)]
-    greet += [{"section": below, "dp": blocks[i]} for i in range(n)]
+
+    def signal(sem, **to):
+        pl.semaphore_signal(sem, inc=1, device_id=to, device_id_type=pl.DeviceIdType.MESH)
+
+    signal(barrier, tensor=pc)
+    signal(barrier, section=below)
     if sections > 2:
-        greet += [{"section": above, "dp": blocks[i]} for i in range(n)]
-    for to in greet:
-        pl.semaphore_signal(barrier, inc=1, device_id=to, device_id_type=pl.DeviceIdType.MESH)
+        signal(barrier, section=above)
+    pl.when(d > 0)(lambda: signal(barrier, dp=d - 1))
+    pl.when(d < n - 1)(lambda: signal(barrier, dp=d + 1))
+    sides = jnp.where(d > 0, 1, 0) + jnp.where(d < n - 1, 1, 0)
     small = [
         pltpu.make_async_copy(source, kept, small_sem.at[i])
         for i, (source, kept) in enumerate(
@@ -176,7 +183,7 @@
     for copy in small:
         copy.start()
 
-    pl.semaphore_wait(barrier, len(greet))
+    pl.semaphore_wait(barrier, sides + (2 if sections == 2 else 3))
 
     part = half // CHUNKS
 
@@ -225,11 +232,24 @@
             own_line(j, d - 1, dn_send).start()
 
     cn_copy.start()
+    pl.when(d == 0)(lambda: signal(low_in, dp=d + 1))
+    pl.when(d == n - 1)(lambda: signal(high_in, dp=d - 1))
     pltpu.make_async_copy(pre_hbm, pre_v, pre_sem).wait()
     for t in range(n_th):
         down_copy(t).start()
     for t in range(n_tn):
         up_copy(t).start()
+
+    @pl.when(d > 0)
+    def _():
+        pl.semaphore_wait(low_in, 1)
+        pl.when(d < n - 1)(lambda: signal(low_in, dp=d + 1))
+
+    @pl.when(d < n - 1)
+    def _():
+        pl.semaphore_wait(high_in, 1)
+        pl.when(d > 0)(lambda: signal(high_in, dp=d - 1))
+
     for copy in small:
         copy.wait()
     block_rows = routes_ref.shape[0]
@@ -243,6 +263,7 @@
                 weight += jnp.where(routes_ref[q, k] == expert, share, 0.0)
         wt_own[p] = weight
 
+    signal(line_in, section=above)
     for i in range(1, n):
         wt_copy(i, d).start()
     own_copy.wait()
@@ -442,6 +463,8 @@
 
             return carry
 
+        if g == 0:
+            pl.semaphore_wait(line_in, 1)
         lax.fori_loop(0, n_tn, second, 0)
         need = min((g + 2) * group - 1, n - 1)
         while g + 1 < n_groups and arrived < need:
@@ -600,7 +623,7 @@
     group = GROUP
     half = tok // 2
     m = group * tok
-    th = tile_of(hidden_cols, 512)
+    th = tile_of(hidden_cols, 896)
     tn = tile_of(width, 512)
     n_th, n_tn, n_g = hidden_cols // th, width // tn, n // group
     dma = pltpu.SemaphoreType.DMA
@@ -667,6 +690,9 @@
             dma(()),
             dma(()),
             dma(()),
+            pltpu.SemaphoreType.REGULAR,
+            pltpu.SemaphoreType.REGULAR,
+            pltpu.SemaphoreType.REGULAR,
             dma((n_tn, SPLIT)),
             pltpu.SMEM(routes.shape[1:], jnp.int32),
             pltpu.VMEM((2, tok), F32),

time: 56.2 us -> 55.9 us (level)
  no operation moved by 1% of the time
where the time goes in v6:
time: 55.9 us; the launch traced here: 55.8 us
  Pallas kernels  55.1 us (99%)
  between operations  0.64 us (1%)
    pallas_call x1, Pallas kernels, per_device(): pl.pallas_call(functools.partial(kernel, n, sections, group, th, tn), out...  53.2 us
    pallas_call x1, Pallas kernels, per_device(): pl.pallas_call(functools.partial(hand_over, PARTS), out_shape=(jax.ShapeD...  1.94 us

profile of v6, /device:TPU:0, one launch (start us, length us, event | category | flops | bytes accessed | tf_op | source)
XLA Modules:
  0.0 55.8 jit_solution(15398340445524675906)
XLA Ops:
  0.6 53.2 %window.1 = (bf16[128,2048]{1,0:T(8,128)(2,1)}, f32[256,128]{1,0:T(8,128)}) custom-call(bf16[128,2048]{1,0:T(8,128)(2,1)} %bitcast.23, s32[1,2]{1,0:T(1,128)} %bitcast.28, f32[2,128]{1,0:T(2,128)} %bitcast.27, bf16[2048,3584]{1,0:T(8,128)(2,1)} %bitcast.20, bf16[3584,2048]{1,0:T(8,128)(2,1)} %bitcast.21, bf16[4,128,3584]{2,1,0:T(8,128)(2,1)} %bitcast.22, ...), custom_call_target="tpu_custom_call" | custom-call | tf_op jit(solution)/shard_map/window/pallas_call | solution.py:631
  53.8 1.9 %hand_over.1 = (bf16[128,2048]{1,0:T(8,128)(2,1)}, f32[256,128]{1,0:T(8,128)}) custom-call(bf16[128,2048]{1,0:T(8,128)(2,1)} %get-tuple-element.6.hand_in, f32[256,128]{1,0:T(8,128)} %get-tuple-element.7.feat_in), custom_call_target="tpu_custom_call" | custom-call | tf_op jit(solution)/shard_map/hand_over/pallas_call | solution.py:721
